TPU v7x, 32 devices: a whole 2x2x4 slice. The times are simulated.
32 devices in a mesh: samp: 4 (over x, core), snp: 4 (over z), gene: 2 (over y).
Axes of the slice: x: 2, y: 2, z: 4, core: 2. Of those that a mesh axis runs over, the one named last changes fastest.
Arguments:
- dosage: bfloat16 [18432, 1024], P(('samp', 'gene'), 'snp'), may hold values from 0 to 2
- snp_scale: float32 [1024], P('snp'), may hold values from 0.5 to 2
- covariates: float32 [18432, 64], P(('samp', 'gene'))
- previous: bfloat16 [18432, 1024], P(('samp', 'gene'), 'snp')
- expression: bfloat16 [18432, 20480], P('samp', 'gene')
Outputs:
- resid: bfloat16 [18432, 1024], P(('samp', 'gene'), 'snp')
- zscores: bfloat16 [1024, 20480], P('snp', 'gene')
All inputs are finite; a program needn't handle non-finite values.
Results may differ from a plain program's by a relative error of at most 0.001.
Values may be sent and summed in bfloat16 or wider, within the bound.
No kernel may reach another device: no remote copies, remote signals or barrier semaphores. Data moves between devices by JAX's collectives and lax.ppermute only.
A program may use at most 192 MiB of HBM per device.

v0:
```python
import jax
import jax.numpy as jnp
from jax import lax
from jax.sharding import PartitionSpec as P


def on_device(dosage, snp_scale, covariates, previous, expression):
    highest = lax.Precision.HIGHEST
    decoded = dosage.astype(jnp.float32) * snp_scale[None, :]
    gram = jnp.dot(covariates.T, covariates, precision=highest)
    cross = jnp.dot(covariates.T, decoded, precision=highest)
    gram, cross = lax.psum((gram, cross), ("samp", "gene"))
    factor = jnp.linalg.cholesky(gram)
    coef = jax.scipy.linalg.cho_solve((factor, True), cross)
    resid = (decoded - jnp.dot(covariates, coef, precision=highest)).astype(jnp.bfloat16)
    piece = lax.all_gather(previous, "gene", axis=0, tiled=True)
    partial_scores = lax.dot_general(
        piece, expression, (((0,), (0,)), ((), ())), preferred_element_type=jnp.float32
    )
    x_sq = jnp.einsum("sp,sp->p", piece, piece, preferred_element_type=jnp.float32)
    scores, x_sq = (partial_scores, x_sq)
    y_sq = jnp.einsum("sg,sg->g", expression, expression, preferred_element_type=jnp.float32)
    samples = expression.shape[0] * lax.axis_size("samp")
    root = jnp.sqrt(jnp.float32(samples))
    shares, y_share = (
        lax.psum_scatter(scores, "samp", scatter_dimension=1, tiled=True),
        lax.psum_scatter(y_sq, "samp", scatter_dimension=0, tiled=True),
    )
    x_sq = lax.psum(x_sq, "samp")
    denom = jnp.sqrt(x_sq + 1e-06)[:, None] * jnp.sqrt(y_share + 1e-06)[None, :]
    z_part = (root * shares / denom).astype(jnp.bfloat16)
    zscores = lax.all_gather(z_part, "samp", axis=1, tiled=True)
    return (resid, zscores)


def solution(mesh):
    placed = (
        P(("samp", "gene"), "snp"),
        P("snp"),
        P(("samp", "gene"), None),
        P(("samp", "gene"), "snp"),
        P("samp", "gene"),
    )
    return jax.shard_map(
        on_device,
        mesh=mesh,
        in_specs=placed,
        out_specs=(P(("samp", "gene"), "snp"), P("snp", "gene")),
        check_vma=False,
    )
```

profile of v0, /device:TPU:0, one launch (start us, length us, event | category | flops | bytes accessed | tf_op | source)
XLA Modules:
  0.0 232.6 jit_solution(6112075205556040852)
XLA Ops:
  8.0 0.0 copy-start
  8.0 0.0 all-gather.3.cloned.1.call-start
  8.1 0.7 all-gather.3.cloned.1.call-update
  8.7 0.0 reduce-scatter.2.cloned.1.call-start
  8.8 40.4 %all-gather.3.cloned.1.call-done = bf16[4608,256]{1,0:T(8,128)(2,1)} async-done(((bf16[2304,256]{1,0:T(8,128)(2,1)}), bf16[4608,256]{1,0:T(8,128)(2,1)}) %all-gather.3.cloned.1.call-update) | async-done | bytes 2359312 | tf_op jit(solution)/shard_map/all_gather | solution.py:16
  49.2 39.2 %fusion.15 = f32[256,10240]{1,0:T(8,128)} fusion(bf16[4608,256]{1,0:T(8,128)(2,1)} %all-gather.3.cloned.1.call-done, bf16[4608,10240]{1,0:T(8,128)(2,1)} %param.9), kind=kOutput, calls=%fused_computation.28 | convolution fusion | flops 24159191040 | bytes 107216896 | tf_op jit(solution)/shard_map/dot_general | solution.py:17
  88.4 0.0 copy-start.1
  88.4 0.0 reduce-scatter.2.cloned.1.call-update
  88.4 0.0 copy-start.2
  88.4 0.0 all-reduce.4.cloned.1.call-start
  88.5 1.2 copy-done.1
  89.6 0.7 copy.11
  90.4 0.0 copy-done
  90.4 0.0 copy-done.2
  90.4 2.7 %fusion.6 = f32[64,256]{0,1:T(8,128)} fusion(f32[2304,64]{0,1:T(8,128)S(1)} %copy-done, bf16[2304,256]{0,1:T(8,128)(2,1)S(1)} %copy.11, f32[256]{0:T(256)S(1)} %copy-done.2), kind=kOutput, calls=%fused_computation.11 | convolution fusion | flops 454164480 | bytes 1836032 | tf_op jit(solution)/shard_map/dot_general | solution.py:11
  93.1 0.0 all-reduce.4.cloned.1.call-update
  93.1 0.0 all-gather.5.cloned.1.call-start
  93.2 0.0 copy-start.3
  93.2 35.1 %fusion = f32[10240]{0:T(1024)S(1)} fusion(bf16[4608,10240]{1,0:T(8,128)(2,1)} %param.9), kind=kLoop, calls=%fused_computation.1 | loop fusion | flops 141547520 | bytes 94412800 | tf_op jit(solution)/shard_map/sg,sg->g/dot_general | solution.py:22
  128.3 0.0 copy-done.3
  128.3 0.6 dynamic-slice
  129.5 2.4 %fusion.1 = f32[256]{0:T(256)S(1)} fusion(bf16[4608,256]{1,0:T(8,128)(2,1)} %all-gather.3.cloned.1.call-done), kind=kLoop, calls=%fused_computation.3 | loop fusion | flops 3538688 | bytes 2360320 | tf_op jit(solution)/shard_map/sp,sp->p/dot_general | solution.py:20
  131.9 13.8 %all-reduce.1 = (f32[10240]{0:T(1024)S(1)}, f32[256]{0:T(256)S(1)}) all-reduce(f32[10240]{0:T(1024)S(1)} %fusion, f32[256]{0:T(256)S(1)} %fusion.1), channel_id=3, replica_groups=mesh['samp'=4,'snp'=4,'gene'=2] {'samp'}, use_global_device_ids=true, to_apply=%region_6.7.clone | all-reduce | flops 10496 | bytes 83968
  145.7 0.1 fusion.13
  145.8 28.1 %reduce-scatter.2.cloned.1.call-done = f32[256,2560]{1,0:T(8,128)} async-done(((f32[256,10240]{1,0:T(8,128)}), f32[256,2560]{1,0:T(8,128)}) %reduce-scatter.2.cloned.1.call-update) | async-done | bytes 2621456 | tf_op jit(solution)/shard_map/reduce_scatter | solution.py:26
  173.9 3.3 %divide_convert_fusion = bf16[256,2560]{1,0:T(8,128)(2,1)} fusion(f32[256,2560]{1,0:T(8,128)} %reduce-scatter.2.cloned.1.call-done, f32[2560]{0:T(1024)S(1)} %fusion.13, f32[256]{0:T(256)S(1)} %add_sqrt_fusion), kind=kLoop, calls=%fused_computation.7 | loop fusion | flops 2621440 | bytes 3943424 | tf_op jit(solution)/shard_map/convert_element_type | solution.py:31
  177.2 0.0 all-gather.5.cloned.1.call-update
  177.2 0.6 fusion.14
  177.9 25.0 %psum.21 = f32[64,64]{0,1:T(8,128)S(1)} all-reduce(f32[64,64]{0,1:T(8,128)S(1)} %fusion.14), channel_id=1, replica_groups=mesh['samp'=4,'snp'=4,'gene'=2] {'samp','gene'}, use_global_device_ids=true, to_apply=%region_0.0 | all-reduce | flops 4096 | bytes 32768 | tf_op jit(solution)/shard_map/psum | solution.py:12
  202.9 0.1 copy.13
  203.0 5.8 %cholesky.16 = f32[64,64]{1,0:T(8,128)S(1)} custom-call(f32[64,64]{1,0:T(8,128)S(1)} %fusion.12), custom_call_target="Cholesky" | custom-call | tf_op jit(solution)/shard_map/jit(cholesky)/cholesky | solution.py:13
  208.9 0.7 compare_reduce_fusion
  209.5 0.6 fusion.7
  210.2 4.9 %custom-call.10 = f32[1,64,64]{1,2,0:T(8,128)S(1)} custom-call(f32[1,64,64]{2,1,0:T(8,128)S(1)} %fusion.7), custom_call_target="InvertDiagBlocksLowerTriangular" | custom-call | tf_op jit(solution)/shard_map/jit(_cho_solve)/triangular_solve | solution.py:14
  215.1 0.0 all-reduce.4.cloned.1.call-done
  215.1 1.2 fusion.10
  216.3 0.2 fusion.8
  216.5 2.1 fusion.3
  218.6 1.4 copy.14
  220.0 0.0 all-gather.5.cloned.1.call-done
  220.0 5.4 %copy.30 = bf16[256,10240]{1,0:T(8,128)(2,1)} copy(bf16[256,10240]{1,0:T(8,128)(2,1)} %all-gather.5.cloned.1.call-done) | data formatting | bytes 10485760
  (3 shorter events, 0.0 us)
Async XLA Ops:
  8.0 82.4 %copy-start = (f32[2304,64]{0,1:T(8,128)S(1)}, f32[2304,64]{0,1:T(8,128)}, u32[]{:S(2)}) copy-start(f32[2304,64]{0,1:T(8,128)} %param.7) | copy-start | bytes 1769476
  8.0 41.2 %all-gather.3.cloned.1.call-start = ((), (), s32[]{:S(2)}) async-start(), calls=%async_computation.2 | async-start | bytes 3538944 | tf_op jit(solution)/shard_map/all_gather | solution.py:16
  8.7 165.2 %reduce-scatter.2.cloned.1.call-start = ((), (), s32[]{:S(2)}) async-start(), calls=%async_computation.3 | async-start | bytes 13107200 | tf_op jit(solution)/shard_map/reduce_scatter | solution.py:26
  88.4 1.3 copy-start.1
  88.4 2.0 copy-start.2
  88.4 126.7 %all-reduce.4.cloned.1.call-start = ((), (), s32[]{:S(2)}) async-start(), calls=%async_computation.1 | async-start | bytes 262144 | tf_op jit(solution)/shard_map/psum | solution.py:12
  93.1 127.0 %all-gather.5.cloned.1.call-start = ((), (), s32[]{:S(2)}) async-start(), calls=%async_computation.4 | async-start | bytes 6553600 | tf_op jit(solution)/shard_map/all_gather | solution.py:32
  93.2 35.1 %copy-start.3 = (u32[32]{0:T(128)S(1)}, u32[32]{0:T(128)}, u32[]{:S(2)}) copy-start(u32[32]{0:T(128)} %constant.58) | copy-start | bytes 388
Sparse Core Ops, SparseCore 0:
  10.4 38.7 all-gather.2
  88.5 85.3 reduce-scatter.1
  177.4 40.6 all-gather.4
Sparse Core Ops, SparseCore 1:
  93.2 121.3 all-reduce.3
where the time goes:
time: 233 us
  waiting for transfers between devices  69.2 us (30%)
  other arithmetic  53 us (23%)
  matrix products  46 us (20%)
  blocking collectives  38.8 us (17%)
  between operations  16 us (7%)
  local copies, waits for them, and re-layouts  9.4 us (4%)
    all_gather x1, waiting for transfers between devices, on_device(): piece = lax.all_gather(previous, 'gene', axis=0, tiled=True)  40.4 us
    dot_general x1, matrix products, on_device(): lax.dot_general(piece, expression, (((0,), (0,)), ((), ())), preferred_el...  39.2 us
    dot_general x1, other arithmetic, on_device(): jnp.einsum('sg,sg->g', expression, expression, preferred_element_type=jnp...  35.1 us
    reduce_scatter x1, waiting for transfers between devices, on_device(): lax.psum_scatter(scores, 'samp', scatter_dimension=1, tiled=True)  28.1 us
    psum x1, blocking collectives, on_device(): gram, cross = lax.psum((gram, cross), ('samp', 'gene'))  25 us
    unnamed x1, blocking collectives  13.8 us
    unnamed x12, local copies, waits for them, and re-layouts  9.32 us
    another operation x3, other arithmetic, on_device(): factor = jnp.linalg.cholesky(gram)  6.55 us
  transfers between devices with their start and end apart: 4, of which 2 were waited for; matrix products, arithmetic and copies ran while one was open for 27% of the time, Pallas kernels for 0%

commit v1 on v0

--- a/solution.py
+++ b/solution.py
@@ -2,6 +2,11 @@
 import jax.numpy as jnp
 from jax import lax
 from jax.sharding import PartitionSpec as P
+
+
+def one_after_other(value, first, second):
+    inner = lax.psum(value, first)
+    return lax.psum(inner, second)
 
 
 def on_device(dosage, snp_scale, covariates, previous, expression):
@@ -9,7 +14,7 @@
     decoded = dosage.astype(jnp.float32) * snp_scale[None, :]
     gram = jnp.dot(covariates.T, covariates, precision=highest)
     cross = jnp.dot(covariates.T, decoded, precision=highest)
-    gram, cross = lax.psum((gram, cross), ("samp", "gene"))
+    gram, cross = one_after_other((gram, cross), "gene", "samp")
     factor = jnp.linalg.cholesky(gram)
     coef = jax.scipy.linalg.cho_solve((factor, True), cross)
     resid = (decoded - jnp.dot(covariates, coef, precision=highest)).astype(jnp.bfloat16)

time: 233 us -> 262 us (1.12)
  waiting for transfers between devices: 69.2 us -> 119 us
  blocking collectives: 38.8 us -> 21.8 us
    all_gather x1, waiting for transfers between devices: 0.01 us -> 37.5 us  [on_device(): zscores = lax.all_gather(z_part, 'samp', axis=1, tiled=True)]
    psum x1 -> x2, waiting for transfers between devices: 0.03 us -> 18.7 us  [the longest x1 18.6 us: one_after_other(): return lax.psum(inner, second)]
    unnamed x1 -> x0, blocking collectives: 13.8 us -> none
    all_gather x1, waiting for transfers between devices: 40.4 us -> 36 us  [on_device(): piece = lax.all_gather(previous, 'gene', axis=0, tiled=True)]
    psum x1 -> x2, blocking collectives: 25 us -> 21.8 us  [the longest x1 14.6 us: one_after_other(): return lax.psum(inner, second)]
    unnamed x12 -> x10, local copies, waits for them, and re-layouts: 9.32 us -> 9.56 us
  transfers between devices with their start and end apart: 4 -> 5, of which waited for: 2 -> 4; matrix products, arithmetic and copies ran while one was open for 27% -> 38% of each run, Pallas kernels for 0% -> 0%
where the time goes in v1:
time: 262 us
  waiting for transfers between devices  119 us (45%)
  other arithmetic  51 us (19%)
  matrix products  46.1 us (18%)
  blocking collectives  21.8 us (8%)
  between operations  14.6 us (6%)
  local copies, waits for them, and re-layouts  9.63 us (4%)
    dot_general x1, matrix products, on_device(): lax.dot_general(piece, expression, (((0,), (0,)), ((), ())), preferred_el...  39.3 us
    all_gather x1, waiting for transfers between devices, on_device(): zscores = lax.all_gather(z_part, 'samp', axis=1, tiled=True)  37.5 us
    all_gather x1, waiting for transfers between devices, on_device(): piece = lax.all_gather(previous, 'gene', axis=0, tiled=True)  36 us
    dot_general x1, other arithmetic, on_device(): jnp.einsum('sg,sg->g', expression, expression, preferred_element_type=jnp...  33.1 us
    reduce_scatter x1, waiting for transfers between devices, on_device(): lax.psum_scatter(scores, 'samp', scatter_dimension=1, tiled=True)  25.8 us
    psum x1, waiting for transfers between devices, one_after_other(): return lax.psum(inner, second)  18.6 us
    psum x1, blocking collectives, one_after_other(): return lax.psum(inner, second)  14.6 us
    unnamed x10, local copies, waits for them, and re-layouts  9.56 us
  transfers between devices with their start and end apart: 5, of which 4 were waited for; matrix products, arithmetic and copies ran while one was open for 38% of the time, Pallas kernels for 0%

profile of v1, /device:TPU:0, one launch (start us, length us, event | category | flops | bytes accessed | tf_op | source)
XLA Modules:
  0.0 261.9 jit_solution(14941296889410369891)
XLA Ops:
  7.2 0.0 copy-start
  7.2 0.0 copy-start.1
  7.2 0.0 all-gather.3.cloned.1.call-start
  7.2 0.7 all-gather.3.cloned.1.call-update
  7.9 0.0 all-reduce.5.cloned.1.call-start
  8.0 1.6 copy.11
  9.5 0.0 copy-done
  9.6 0.0 copy-done.1
  9.6 2.7 %fusion.6 = f32[64,256]{0,1:T(8,128)} fusion(f32[2304,64]{0,1:T(8,128)S(1)} %copy-done, bf16[2304,256]{0,1:T(8,128)(2,1)S(1)} %copy.11, f32[256]{0:T(256)S(1)} %copy-done.1), kind=kOutput, calls=%fused_computation.11 | convolution fusion | flops 454164480 | bytes 1836032 | tf_op jit(solution)/shard_map/dot_general | solution.py:16
  12.3 0.0 all-reduce.5.cloned.1.call-update
  12.3 0.0 reduce-scatter.2.cloned.1.call-start
  12.3 36.0 %all-gather.3.cloned.1.call-done = bf16[4608,256]{1,0:T(8,128)(2,1)} async-done(((bf16[2304,256]{1,0:T(8,128)(2,1)}), bf16[4608,256]{1,0:T(8,128)(2,1)}) %all-gather.3.cloned.1.call-update) | async-done | bytes 2359312 | tf_op jit(solution)/shard_map/all_gather | solution.py:21
  48.3 39.3 %fusion.15 = f32[256,10240]{1,0:T(8,128)} fusion(bf16[4608,256]{1,0:T(8,128)(2,1)} %all-gather.3.cloned.1.call-done, bf16[4608,10240]{1,0:T(8,128)(2,1)} %param.9), kind=kOutput, calls=%fused_computation.28 | convolution fusion | flops 24159191040 | bytes 107216896 | tf_op jit(solution)/shard_map/dot_general | solution.py:22
  87.6 0.0 copy-start.2
  87.6 0.0 reduce-scatter.2.cloned.1.call-update
  87.7 0.0 all-reduce.7.cloned.1.call-start
  87.7 0.6 copy-done.2
  88.3 0.6 dynamic-slice
  89.5 0.6 fusion.14
  90.1 7.2 %psum.35 = f32[64,64]{0,1:T(8,128)S(1)} all-reduce(f32[64,64]{0,1:T(8,128)S(1)} %fusion.14), channel_id=1, replica_groups=mesh['samp'=4,'snp'=4,'gene'=2] {'gene'}, use_global_device_ids=true, to_apply=%region_0.0 | all-reduce | flops 4096 | bytes 32768 | tf_op jit(solution)/shard_map/psum | solution.py:8
  97.3 33.1 %fusion = f32[10240]{0:T(1024)S(1)} fusion(bf16[4608,10240]{1,0:T(8,128)(2,1)} %param.9), kind=kLoop, calls=%fused_computation.1 | loop fusion | flops 141547520 | bytes 94412800 | tf_op jit(solution)/shard_map/sg,sg->g/dot_general | solution.py:27
  130.5 0.0 all-reduce.5.cloned.1.call-done
  130.5 0.0 all-reduce.7.cloned.1.call-update
  130.5 0.0 all-gather.5.cloned.1.call-start
  130.6 2.4 fusion.1
  132.9 14.6 %all-reduce.1 = (f32[64,64]{0,1:T(8,128)S(1)}, f32[10240]{0:T(1024)S(1)}, f32[256]{0:T(256)S(1)}) all-reduce(f32[64,64]{0,1:T(8,128)S(1)} %psum.35, f32[10240]{0:T(1024)S(1)} %fusion, f32[256]{0:T(256)S(1)} %fusion.1), channel_id=1, replica_groups=mesh['samp'=4,'snp'=4,'gene'=2] {'samp'}, use_global_device_ids=true, to_apply=%region_1.0 | all-reduce | flops 14592 | bytes 116736 | tf_op jit(solution)/shard_map/psum | solution.py:9
  147.5 0.1 fusion.13
  147.6 25.8 %reduce-scatter.2.cloned.1.call-done = f32[256,2560]{1,0:T(8,128)} async-done(((f32[256,10240]{1,0:T(8,128)}), f32[256,2560]{1,0:T(8,128)}) %reduce-scatter.2.cloned.1.call-update) | async-done | bytes 2621456 | tf_op jit(solution)/shard_map/reduce_scatter | solution.py:31
  173.4 3.3 %divide_convert_fusion = bf16[256,2560]{1,0:T(8,128)(2,1)} fusion(f32[256,2560]{1,0:T(8,128)} %reduce-scatter.2.cloned.1.call-done, f32[2560]{0:T(1024)S(1)} %fusion.13, f32[256]{0:T(256)S(1)} %add_sqrt_fusion), kind=kLoop, calls=%fused_computation.7 | loop fusion | flops 2621440 | bytes 3943424 | tf_op jit(solution)/shard_map/convert_element_type | solution.py:36
  176.7 0.0 all-gather.5.cloned.1.call-update
  176.8 0.1 copy.13
  176.9 5.8 %cholesky.16 = f32[64,64]{1,0:T(8,128)S(1)} custom-call(f32[64,64]{1,0:T(8,128)S(1)} %fusion.12), custom_call_target="Cholesky" | custom-call | tf_op jit(solution)/shard_map/jit(cholesky)/cholesky | solution.py:18
  182.7 0.6 compare_reduce_fusion
  183.4 0.7 fusion.7
  184.1 4.9 %custom-call.10 = f32[1,64,64]{1,2,0:T(8,128)S(1)} custom-call(f32[1,64,64]{2,1,0:T(8,128)S(1)} %fusion.7), custom_call_target="InvertDiagBlocksLowerTriangular" | custom-call | tf_op jit(solution)/shard_map/jit(_cho_solve)/triangular_solve | solution.py:19
  188.9 18.6 %all-reduce.7.cloned.1.call-done = f32[64,256]{0,1:T(8,128)} async-done(((f32[64,256]{0,1:T(8,128)}), f32[64,256]{0,1:T(8,128)}) %all-reduce.7.cloned.1.call-update) | async-done | bytes 65552 | tf_op jit(solution)/shard_map/psum | solution.py:9
  207.6 1.2 fusion.10
  208.8 0.2 fusion.8
  209.0 2.1 fusion.3
  211.1 1.4 copy.14
  212.5 37.5 %all-gather.5.cloned.1.call-done = bf16[256,10240]{1,0:T(8,128)(2,1)} async-done(((bf16[256,2560]{1,0:T(8,128)(2,1)}), bf16[256,10240]{1,0:T(8,128)(2,1)}) %all-gather.5.cloned.1.call-update) | async-done | bytes 5242896 | tf_op jit(solution)/shard_map/all_gather | solution.py:37
  250.0 5.4 %copy.31 = bf16[256,10240]{1,0:T(8,128)(2,1)} copy(bf16[256,10240]{1,0:T(8,128)(2,1)} %all-gather.5.cloned.1.call-done) | data formatting | bytes 10485760
  (3 shorter events, 0.0 us)
Async XLA Ops:
  7.2 2.4 copy-start
  7.2 2.4 copy-start.1
  7.2 41.2 %all-gather.3.cloned.1.call-start = ((), (), s32[]{:S(2)}) async-start(), calls=%async_computation.3 | async-start | bytes 3538944 | tf_op jit(solution)/shard_map/all_gather | solution.py:21
  7.9 122.6 %all-reduce.5.cloned.1.call-start = ((), (), s32[]{:S(2)}) async-start(), calls=%async_computation.1 | async-start | bytes 262144 | tf_op jit(solution)/shard_map/psum | solution.py:8
  12.3 161.2 %reduce-scatter.2.cloned.1.call-start = ((), (), s32[]{:S(2)}) async-start(), calls=%async_computation.4 | async-start | bytes 13107200 | tf_op jit(solution)/shard_map/reduce_scatter | solution.py:31
  87.6 0.7 copy-start.2
  87.7 119.9 %all-reduce.7.cloned.1.call-start = ((), (), s32[]{:S(2)}) async-start(), calls=%async_computation.2 | async-start | bytes 262144 | tf_op jit(solution)/shard_map/psum | solution.py:9
  130.5 119.5 %all-gather.5.cloned.1.call-start = ((), (), s32[]{:S(2)}) async-start(), calls=%async_computation.5 | async-start | bytes 6553600 | tf_op jit(solution)/shard_map/all_gather | solution.py:37
Sparse Core Ops, SparseCore 0:
  9.5 38.7 all-gather.2
  51.2 21.5 all-reduce.4
  87.8 85.6 reduce-scatter.1
  175.6 31.9 all-reduce.6
  209.6 40.3 all-gather.4
